TPU v7x, 256 devices: a whole 4x4x8 slice. The times are simulated.
256 devices in a mesh: ctx: 64 (over z, x_hi, y), tp: 4 (over x_lo, core).
Axes of the slice: x: 4 (x_hi: 2, x_lo: 2; x = x_hi * 2 + x_lo), y: 4, z: 8, core: 2. Of those that a mesh axis runs over, the one named last changes fastest.
Arguments:
- queries: bfloat16 [9216, 3072], P('ctx', 'tp'), may hold values from -8 to 8
- keys: bfloat16 [9216, 3072], P('ctx', 'tp'), may hold values from -8 to 8
- values: bfloat16 [9216, 3072], P('ctx', 'tp'), may hold values from -6 to 6
- positions: int32 [9216], P('ctx'), may hold values from 0 to 9215, as said below
- lambda_vecs: float32 [4, 12, 128], P(None, 'tp'), may hold values from -0.6 to 0.6
- head_gain: float32 [3072], P('tp'), may hold values from 0.5 to 1.5
- out_weight: bfloat16 [3072, 5120], P('tp'), may hold values from -0.109375 to 0.109375
- residual: bfloat16 [9216, 5120], P('ctx', 'tp'), may hold values from -3 to 3
Outputs:
- mixed: bfloat16 [9216, 5120], P('ctx', 'tp')
Inputs may be any that keep to these rules, and one draw needn't show every extreme that they name: Each aligned run of 72 rows holds 72 consecutive positions in increasing order; the runs' first positions are the multiples of 72, each once.
All inputs are finite; a program needn't handle non-finite values.
Results may differ from a plain program's by a relative error of at most 0.012.
Values may be sent and summed in bfloat16 or wider, within the bound.
No kernel may reach another device: no remote copies, remote signals or barrier semaphores. Data moves between devices by JAX's collectives and lax.ppermute only.
A program may use at most 192 MiB of HBM per device.

v0:
```python
import math
import jax
import jax.numpy as jnp
from jax import lax
from jax.sharding import PartitionSpec as P

lambda_init = 0.2
out_factor = 0.8
norm_eps = 1e-05


def per_device(queries, keys, values, positions, lambda_vecs, head_gain, out_weight, residual):
    row_count = queries.shape[0]
    head_count = lambda_vecs.shape[1]
    head_depth = lambda_vecs.shape[2]
    score_scale = 1.0 / math.sqrt(head_depth)
    query_heads = queries.reshape(row_count, head_count, 2, head_depth)
    all_positions = lax.all_gather(positions, "ctx", axis=0, tiled=True)
    key_piece = lax.all_gather(keys, "ctx", axis=0, tiled=True)
    value_piece = lax.all_gather(values, "ctx", axis=0, tiled=True)
    piece_rows = key_piece.shape[0]
    allowed = all_positions[None, :] <= positions[:, None]
    highest = jnp.full((2, head_count, row_count), -1e30, jnp.float32)
    scores = (
        jnp.einsum(
            "ihad,jhad->ahij",
            query_heads,
            key_piece.reshape(piece_rows, head_count, 2, head_depth),
            preferred_element_type=jnp.float32,
        )
        * score_scale
    )
    scores = jnp.where(allowed, scores, -jnp.inf)
    fresh = jnp.maximum(highest, jnp.max(scores, -1))
    expo = jnp.where(allowed, jnp.exp(scores - fresh[..., None]), 0.0)
    total = jnp.sum(expo, -1)
    numerator = jnp.einsum(
        "ahij,jhe->ahie",
        expo.astype(jnp.bfloat16),
        value_piece.reshape(piece_rows, head_count, 2 * head_depth),
        preferred_element_type=jnp.float32,
    )
    highest, total, numerator = (fresh, total, numerator)
    attn = numerator / total[..., None]
    lambda_head = (
        jnp.exp(jnp.sum(lambda_vecs[0] * lambda_vecs[1], -1))
        - jnp.exp(jnp.sum(lambda_vecs[2] * lambda_vecs[3], -1))
        + lambda_init
    )
    diff = attn[0] - lambda_head[:, None, None] * attn[1]
    mean_square = jnp.mean(diff * diff, -1, keepdims=True)
    normed = (
        out_factor
        * diff
        / jnp.sqrt(mean_square + norm_eps)
        * head_gain.reshape(head_count, 1, 2 * head_depth)
    )
    normed = (
        jnp.transpose(normed, (1, 0, 2))
        .reshape(row_count, head_count * 2 * head_depth)
        .astype(jnp.bfloat16)
    )
    shares = lax.psum_scatter(
        lax.dot_general(
            out_weight, normed, (((0,), (1,)), ((), ())), preferred_element_type=jnp.float32
        ).astype(jnp.bfloat16),
        "tp",
        scatter_dimension=0,
        tiled=True,
    ).astype(jnp.float32)
    projected = jnp.transpose(shares)
    return (projected + residual.astype(jnp.float32)).astype(jnp.bfloat16)


def solution(mesh):
    placed = (
        P("ctx", "tp"),
        P("ctx", "tp"),
        P("ctx", "tp"),
        P("ctx"),
        P(None, "tp", None),
        P("tp"),
        P("tp", None),
        P("ctx", "tp"),
    )
    return jax.shard_map(
        per_device, mesh=mesh, in_specs=placed, out_specs=P("ctx", "tp"), check_vma=False
    )
```

profile of v0, /device:TPU:1, one launch (start us, length us, event | category | flops | bytes accessed | tf_op | source)
XLA Modules:
  0.0 507.1 jit_solution(6777662970282332329)
XLA Ops:
  6.5 0.7 all-gather.3.cloned.1.call-update
  7.3 0.0 all-gather.5.cloned.1.call-start
  7.3 0.7 all-gather.5.cloned.1.call-update
  8.0 0.0 reduce-scatter.2.cloned.1.call-start
  8.1 1.0 reshape.37
  9.1 0.7 mul.50
  9.8 1.3 dynamic-slice
  11.7 0.9 dynamic-update-slice
  12.6 310.0 %all-reduce = s32[9216]{0:T(1024)S(1)} all-reduce(s32[9216]{0:T(1024)S(1)} %dynamic-update-slice), channel_id=1, replica_groups=mesh['ctx'=64,'tp'=4] {'ctx'}, use_global_device_ids=true, to_apply=%add | all-reduce | flops 9216 | bytes 73728
  322.6 0.9 multiply_reduce_fusion.2
  323.6 1.4 broadcast_compare_fusion
  325.0 0.0 all-gather.3.cloned.1.call-done
  325.0 18.7 %copy.20 = bf16[9216,768]{0,1:T(8,128)(2,1)} copy(bf16[9216,768]{1,0:T(8,128)(2,1)} %all-gather.3.cloned.1.call-done) | data formatting | bytes 28311552 | tf_op jit(solution)/shard_map/all_gather | solution.py:19
  343.7 16.2 %fusion = (f32[2,3,144]{2,1,0:T(4,128)S(1)}, f32[2,3,144,9216]{3,2,1,0:T(8,128)}) fusion(pred[144,9216]{1,0:T(8,128)(4,1)S(1)} %broadcast_compare_fusion, bf16[9216,3,2,128]{0,3,2,1:T(8,128)(2,1)} %bitcast.44, bf16[144,3,2,128]{3,2,1,0:T(2,128)(2,1)S(1)} %reshape.37), kind=kOutput, calls=%fused_computation.2 | convolution fusion | flops 2062318720 | bytes 47558016 | tf_op jit(solution)/shard_map/ihad,jhad->ahij/dot_general | solution.py:25
  359.9 20.7 %fusion.1 = (f32[2,3,144]{2,1,0:T(4,128)S(1)}, bf16[2,3,144,9216]{3,2,1,0:T(8,128)(2,1)}) fusion(f32[2,3,144,9216]{3,2,1,0:T(8,128)} %get-tuple-element.10, f32[2,3,144]{2,1,0:T(4,128)S(1)} %broadcast_maximum_fusion, pred[144,9216]{1,0:T(8,128)(4,1)S(1)} %broadcast_compare_fusion), kind=kLoop, calls=%fused_computation.3 | loop fusion | flops 47774880 | bytes 49109760 | tf_op jit(solution)/shard_map/reduce_sum | solution.py:36
  380.6 16.6 %all-gather.5.cloned.1.call-done = bf16[9216,768]{1,0:T(8,128)(2,1)} async-done(((bf16[144,768]{1,0:T(8,128)(2,1)}), bf16[9216,768]{1,0:T(8,128)(2,1)}) %all-gather.5.cloned.1.call-update) | async-done | bytes 14155792 | tf_op jit(solution)/shard_map/all_gather | solution.py:20
  397.2 17.8 %copy.23 = bf16[9216,768]{0,1:T(8,128)(2,1)} copy(bf16[9216,768]{1,0:T(8,128)(2,1)} %all-gather.5.cloned.1.call-done) | data formatting | bytes 28311552 | tf_op jit(solution)/shard_map/all_gather | solution.py:20
  415.0 20.3 %fusion.11 = f32[2,3,144,256]{3,2,0,1:T(8,128)S(1)} fusion(bf16[9216,3,256,1]{0,2,3,1:T(8,128)(2,1)} %bitcast.45, bf16[2,3,144,9216]{3,2,1,0:T(8,128)(2,1)} %get-tuple-element.8, f32[2,3,144]{2,0,1:T(2,128)S(1)} %copy.26), kind=kOutput, calls=%fused_computation.13 | convolution fusion | flops 4077084672 | bytes 30969216 | tf_op jit(solution)/shard_map/ahij,jhe->ahie/dot_general | solution.py:37
  435.3 0.3 multiply_reduce_fusion
  435.5 0.2 fusion.18
  435.7 5.7 %fusion.7 = bf16[5120,144]{0,1:T(8,128)(2,1)} fusion(bf16[144,768]{1,0:T(8,128)(2,1)S(1)} %bitcast.46, bf16[768,5120]{1,0:T(8,128)(2,1)} %param.14), kind=kOutput, calls=%fused_computation.10 | convolution fusion | flops 1133199360 | bytes 9560064 | tf_op jit(solution)/shard_map/dot_general | solution.py:64
  441.5 0.0 reduce-scatter.2.cloned.1.call-update
  441.5 57.3 %reduce-scatter.2.cloned.1.call-done = bf16[1280,144]{0,1:T(8,128)(2,1)} async-done(((bf16[5120,144]{0,1:T(8,128)(2,1)}), bf16[1280,144]{0,1:T(8,128)(2,1)}) %reduce-scatter.2.cloned.1.call-update) | async-done | bytes 368656 | tf_op jit(solution)/shard_map/reduce_scatter | solution.py:63
  498.8 1.8 fusion.14
  (9 shorter events, 0.1 us)
Async XLA Ops:
  6.5 318.5 %all-gather.3.cloned.1.call-start = ((), (), s32[]{:S(2)}) async-start(), calls=%async_computation.1 | async-start | bytes 14376960 | tf_op jit(solution)/shard_map/all_gather | solution.py:19
  7.3 390.0 %all-gather.5.cloned.1.call-start = ((), (), s32[]{:S(2)}) async-start(), calls=%async_computation.2 | async-start | bytes 14376960 | tf_op jit(solution)/shard_map/all_gather | solution.py:20
  8.0 490.8 %reduce-scatter.2.cloned.1.call-start = ((), (), s32[]{:S(2)}) async-start(), calls=%async_computation.3 | async-start | bytes 1843200 | tf_op jit(solution)/shard_map/reduce_scatter | solution.py:63
  435.2 63.5 %copy-start = (bf16[144,1280]{1,0:T(8,128)(2,1)S(1)}, bf16[144,1280]{1,0:T(8,128)(2,1)}, u32[]{:S(2)}) copy-start(bf16[144,1280]{1,0:T(8,128)(2,1)} %param.15) | copy-start | bytes 1105924
Sparse Core Ops, SparseCore 0:
  11.0 194.6 all-gather.2
  209.4 187.7 all-gather.4
  441.6 57.1 reduce-scatter.1
where the time goes:
time: 508 us; the launch traced here: 507 us
  blocking collectives  310 us (61%)
  waiting for transfers between devices  75.3 us (15%)
  matrix products  42.2 us (8%)
  local copies, waits for them, and re-layouts  40.3 us (8%)
  other arithmetic  25.4 us (5%)
  between operations  13.8 us (3%)
    unnamed x1, blocking collectives  310 us
    reduce_scatter x1, waiting for transfers between devices, per_device(): lax.psum_scatter(lax.dot_general(out_weight, normed, (((0,), (1,)), ((),...  57.3 us
    reduce_sum x1, other arithmetic, per_device(): total = jnp.sum(expo, -1)  20.7 us
    dot_general x1, matrix products, per_device(): jnp.einsum('ahij,jhe->ahie', expo.astype(jnp.bfloat16), value_piece.resha...  20.3 us
    all_gather x1, local copies, waits for them, and re-layouts, per_device(): key_piece = lax.all_gather(keys, 'ctx', axis=0, tiled=True)  18.7 us
    all_gather x1, local copies, waits for them, and re-layouts, per_device(): value_piece = lax.all_gather(values, 'ctx', axis=0, tiled=True)  17.8 us
    all_gather x1, waiting for transfers between devices, per_device(): value_piece = lax.all_gather(values, 'ctx', axis=0, tiled=True)  16.6 us
    dot_general x1, matrix products, per_device(): jnp.einsum('ihad,jhad->ahij', query_heads, key_piece.reshape(piece_rows,...  16.2 us
  transfers between devices with their start and end apart: 3, of which 2 were waited for; matrix products, arithmetic and copies ran while one was open for 12% of the time, Pallas kernels for 0%

commit v1 on v0

--- a/solution.py
+++ b/solution.py
@@ -16,7 +16,9 @@
     score_scale = 1.0 / math.sqrt(head_depth)
     query_heads = queries.reshape(row_count, head_count, 2, head_depth)
     all_positions = lax.all_gather(positions, "ctx", axis=0, tiled=True)
-    key_piece = lax.all_gather(keys, "ctx", axis=0, tiled=True)
+    key_piece = jnp.concatenate(
+        lax.all_to_all(jnp.stack([keys] * lax.axis_size("ctx")), "ctx", 0, 0), axis=0
+    )
     value_piece = lax.all_gather(values, "ctx", axis=0, tiled=True)
     piece_rows = key_piece.shape[0]
     allowed = all_positions[None, :] <= positions[:, None]

time: 508 us -> 873 us (1.72)
  blocking collectives: 310 us -> 645 us
  starting transfers between devices: 0.08 us -> 15.6 us
  local copies, waits for them, and re-layouts: 40.3 us -> 52.8 us
    unnamed x1, blocking collectives: 310 us -> 645 us
    another operation x0 -> x2, local copies, waits for them, and re-layouts: none -> 34 us  [the longest x1 27 us: per_device(): key_piece.reshape(piece_rows, head_count, 2, head_depth)]
    all_gather x1 -> x0, local copies, waits for them, and re-layouts: 18.7 us -> none  [per_device(): key_piece = lax.all_gather(keys, 'ctx', axis=0, tiled=True)]
    reduce_scatter x1, waiting for transfers between devices: 57.3 us -> 74.4 us  [per_device(): lax.psum_scatter(lax.dot_general(out_weight, normed, (((0,), (1,)), ((),...]
    all_gather x1, waiting for transfers between devices: 16.6 us -> 0.01 us  [per_device(): value_piece = lax.all_gather(values, 'ctx', axis=0, tiled=True)]
    all_to_all x0 -> x1, starting transfers between devices: none -> 15.5 us  [per_device(): lax.all_to_all(jnp.stack([keys] * lax.axis_size('ctx')), 'ctx', 0, 0)]
  transfers between devices with their start and end apart: 3 -> 3, of which waited for: 2 -> 1; matrix products, arithmetic and copies ran while one was open for 12% -> 8% of each run, Pallas kernels for 0% -> 0%
where the time goes in v1:
time: 873 us; the launch traced here: 872 us
  blocking collectives  645 us (74%)
  waiting for transfers between devices  75.2 us (9%)
  local copies, waits for them, and re-layouts  52.8 us (6%)
  matrix products  45 us (5%)
  other arithmetic  23.7 us (3%)
  starting transfers between devices  15.6 us (2%)
  between operations  14.2 us (2%)
    unnamed x1, blocking collectives  645 us
    reduce_scatter x1, waiting for transfers between devices, per_device(): lax.psum_scatter(lax.dot_general(out_weight, normed, (((0,), (1,)), ((),...  74.4 us
    another operation x1, local copies, waits for them, and re-layouts, per_device(): key_piece.reshape(piece_rows, head_count, 2, head_depth)  27 us
    reduce_sum x1, other arithmetic, per_device(): total = jnp.sum(expo, -1)  20.5 us
    dot_general x1, matrix products, per_device(): jnp.einsum('ahij,jhe->ahie', expo.astype(jnp.bfloat16), value_piece.resha...  20.3 us
    dot_general x1, matrix products, per_device(): jnp.einsum('ihad,jhad->ahij', query_heads, key_piece.reshape(piece_rows,...  19 us
    all_gather x1, local copies, waits for them, and re-layouts, per_device(): value_piece = lax.all_gather(values, 'ctx', axis=0, tiled=True)  17.8 us
  transfers between devices with their start and end apart: 3, of which 1 were waited for; matrix products, arithmetic and copies ran while one was open for 8% of the time, Pallas kernels for 0%

profile of v1, /device:TPU:1, one launch (start us, length us, event | category | flops | bytes accessed | tf_op | source)
XLA Modules:
  0.0 871.5 jit_solution(13847423320329387765)
XLA Ops:
  6.5 7.0 stack.2
  13.5 0.0 copy-start.2
  13.5 15.5 %all-to-all-start = ((bf16[64,144,768]{2,1,0:T(8,128)(2,1)}), bf16[64,144,768]{2,1,0:T(8,128)(2,1)}, u32[]{:S(2)}, u32[]{:S(2)}) async-start(bf16[64,144,768]{2,1,0:T(8,128)(2,1)} %stack.2), calls=%async_computation | async-start | bytes 28311552 | tf_op jit(solution)/shard_map/all_to_all | solution.py:20
  29.0 0.0 all-gather.2.cloned.1.call-start
  29.1 0.7 all-gather.2.cloned.1.call-update
  29.8 0.0 reduce-scatter.2.cloned.1.call-start
  29.8 0.1 reshape.36
  29.9 0.6 dynamic-slice
  31.2 0.3 dynamic-update-slice
  31.5 645.1 %all-reduce = s32[9216]{0:T(1024)S(1)} all-reduce(s32[9216]{0:T(1024)S(1)} %dynamic-update-slice), channel_id=1, replica_groups=mesh['ctx'=64,'tp'=4] {'ctx'}, use_global_device_ids=true, to_apply=%add | all-reduce | flops 9216 | bytes 73728
  676.6 0.1 multiply_reduce_fusion.2
  676.7 0.8 broadcast_compare_fusion
  677.5 27.0 %reshape_reshape.3 = bf16[9216,3,2,128]{3,2,1,0:T(2,128)(2,1)} reshape(bf16[64,144,768]{2,1,0:T(8,128)(2,1)} %all-to-all-done) | data formatting | bytes 28311552 | tf_op jit(solution)/shard_map/reshape;reshape | solution.py:30
  704.5 19.0 %fusion = (f32[2,3,144]{2,1,0:T(4,128)S(1)}, f32[2,3,144,9216]{3,2,1,0:T(8,128)}) fusion(pred[144,9216]{1,0:T(8,128)(4,1)S(1)} %broadcast_compare_fusion, bf16[9216,3,2,128]{3,2,1,0:T(2,128)(2,1)} %reshape_reshape.3, bf16[144,3,2,128]{3,2,1,0:T(2,128)(2,1)S(1)} %reshape.36), kind=kOutput, calls=%fused_computation.2 | convolution fusion | flops 2062318720 | bytes 47558016 | tf_op jit(solution)/shard_map/ihad,jhad->ahij/dot_general | solution.py:27
  723.6 20.5 %fusion.1 = (f32[2,3,144]{2,1,0:T(4,128)S(1)}, bf16[2,3,144,9216]{3,2,1,0:T(8,128)(2,1)}) fusion(f32[2,3,144,9216]{3,2,1,0:T(8,128)} %get-tuple-element.10, f32[2,3,144]{2,1,0:T(4,128)S(1)} %broadcast_maximum_fusion, pred[144,9216]{1,0:T(8,128)(4,1)S(1)} %broadcast_compare_fusion), kind=kLoop, calls=%fused_computation.3 | loop fusion | flops 47774880 | bytes 49109760 | tf_op jit(solution)/shard_map/reduce_sum | solution.py:38
  744.1 0.0 all-gather.2.cloned.1.call-done
  744.1 17.8 %copy.21 = bf16[9216,768]{0,1:T(8,128)(2,1)} copy(bf16[9216,768]{1,0:T(8,128)(2,1)} %all-gather.2.cloned.1.call-done) | data formatting | bytes 28311552 | tf_op jit(solution)/shard_map/all_gather | solution.py:22
  761.9 20.3 %fusion.11 = f32[2,3,144,256]{3,2,0,1:T(8,128)S(1)} fusion(bf16[9216,3,256,1]{0,2,3,1:T(8,128)(2,1)} %bitcast.43, bf16[2,3,144,9216]{3,2,1,0:T(8,128)(2,1)} %get-tuple-element.8, f32[2,3,144]{2,0,1:T(2,128)S(1)} %copy.24), kind=kOutput, calls=%fused_computation.13 | convolution fusion | flops 4077084672 | bytes 30969216 | tf_op jit(solution)/shard_map/ahij,jhe->ahie/dot_general | solution.py:39
  782.2 0.3 multiply_reduce_fusion
  782.4 0.2 fusion.18
  782.6 5.7 fusion.7
  788.4 0.0 reduce-scatter.2.cloned.1.call-update
  788.4 74.4 %reduce-scatter.2.cloned.1.call-done = bf16[1280,144]{0,1:T(8,128)(2,1)} async-done(((bf16[5120,144]{0,1:T(8,128)(2,1)}), bf16[1280,144]{0,1:T(8,128)(2,1)}) %reduce-scatter.2.cloned.1.call-update) | async-done | bytes 368656 | tf_op jit(solution)/shard_map/reduce_scatter | solution.py:65
  862.9 1.8 fusion.14
  (19 shorter events, 0.1 us)
Async XLA Ops:
  13.5 16.3 %copy-start.1 = (bf16[144,768]{1,0:T(8,128)(2,1)S(1)}, bf16[144,768]{1,0:T(8,128)(2,1)}, u32[]{:S(2)}) copy-start(bf16[144,768]{1,0:T(8,128)(2,1)} %param.8) | copy-start | bytes 663556
  13.5 16.4 %copy-start.4 = (f32[768]{0:T(1024)S(1)}, f32[768]{0:T(1024)}, u32[]{:S(2)}) copy-start(f32[768]{0:T(1024)} %param.13) | copy-start | bytes 9220
  13.5 16.4 %copy-start.5 = (u32[256]{0:T(256)S(1)}, u32[256]{0:T(256)}, u32[]{:S(2)}) copy-start(u32[256]{0:T(256)} %constant.25) | copy-start | bytes 3076
  13.5 17.7 %copy-start.3 = (s32[144]{0:T(256)S(1)}, s32[144]{0:T(256)}, u32[]{:S(2)}) copy-start(s32[144]{0:T(256)} %param.11) | copy-start | bytes 1732
  13.5 663.1 %copy-start.2 = (f32[4,3,128]{2,0,1:T(4,128)S(1)}, f32[4,3,128]{2,0,1:T(4,128)}, u32[]{:S(2)}) copy-start(f32[4,3,128]{2,0,1:T(4,128)} %param.12) | copy-start | bytes 18436
  13.5 664.0 %all-to-all-start = ((bf16[64,144,768]{2,1,0:T(8,128)(2,1)}), bf16[64,144,768]{2,1,0:T(8,128)(2,1)}, u32[]{:S(2)}, u32[]{:S(2)}) async-start(bf16[64,144,768]{2,1,0:T(8,128)(2,1)} %stack.2), calls=%async_computation | async-start | bytes 28311552 | tf_op jit(solution)/shard_map/all_to_all | solution.py:20
  29.0 715.1 %all-gather.2.cloned.1.call-start = ((), (), s32[]{:S(2)}) async-start(), calls=%async_computation.2 | async-start | bytes 14376960 | tf_op jit(solution)/shard_map/all_gather | solution.py:22
  29.8 833.1 %reduce-scatter.2.cloned.1.call-start = ((), (), s32[]{:S(2)}) async-start(), calls=%async_computation.3 | async-start | bytes 1843200 | tf_op jit(solution)/shard_map/reduce_scatter | solution.py:65
  782.2 80.7 %copy-start = (bf16[144,1280]{1,0:T(8,128)(2,1)S(1)}, bf16[144,1280]{1,0:T(8,128)(2,1)}, u32[]{:S(2)}) copy-start(bf16[144,1280]{1,0:T(8,128)(2,1)} %param.15) | copy-start | bytes 1105924
Sparse Core Ops, SparseCore 0:
  33.5 379.2 all-gather.1
  788.5 74.2 reduce-scatter.1
